TPU v7x, 32 devices: a whole 2x2x4 slice. The times are simulated.
32 devices in a mesh: dp: 8 (over y, x, core), seq: 4 (over z).
Axes of the slice: x: 2, y: 2, z: 4, core: 2. Of those that a mesh axis runs over, the one named last changes fastest.
Arguments:
- tokens: bfloat16 [8, 2048, 768], P('dp', 'seq'), may hold values from -6 to 6
- cotangent: bfloat16 [8, 2048, 768], P('dp', 'seq'), may hold values from -6 to 6
- segment_ids: int32 [8, 2048], P('dp', 'seq'), may hold values from 0 to 7, as said below
- doc_starts: int32 [8, 2048], P('dp', 'seq'), may hold values from 0 to 1, as said below
- valid_mask: int32 [8, 2048], P('dp', 'seq'), may hold values from 0 to 1
- step_number: int32 [1], replicated, may hold values from 1 to 64
- learn_rate: float32 [1], replicated, may hold values from 0.001 to 0.004
- norm_gain: float32 [768], replicated, may hold values from 0.5 to 1.5
- in_weight: bfloat16 [768, 3352], replicated, may hold values from -0.21875 to 0.21875
- conv_weight: float32 [4, 1792], replicated, may hold values from -3 to 3
- conv_bias: float32 [1792], replicated, may hold values from -1.75 to 1.75
- dt_bias: float32 [24], replicated, may hold values from -6 to -2
- a_log: float32 [24], replicated, may hold values from -1 to 2.5
- skip_d: float32 [24], replicated, may hold values from 0.5 to 1.5
- gate_gain: float32 [1536], replicated, may hold values from 0.5 to 1.5
- out_weight: bfloat16 [1536, 768], replicated, may hold values from -0.15625 to 0.15625
- in_momentum: float32 [768, 3352], P('seq'), may hold values from -6 to 6
- out_momentum: float32 [1536, 768], P(None, 'seq'), may hold values from -448 to 448
Outputs:
- output: bfloat16 [8, 2048, 768], P('dp', 'seq')
- input_grad: bfloat16 [8, 2048, 768], P('dp', 'seq')
- new_in_weight: bfloat16 [768, 3352], replicated
- new_out_weight: bfloat16 [1536, 768], replicated
- new_in_momentum: float32 [768, 3352], P('seq')
- new_out_momentum: float32 [1536, 768], P(None, 'seq')
- norm_gain_grad: float32 [768], replicated
- conv_weight_grad: float32 [4, 1792], replicated
- conv_bias_grad: float32 [1792], replicated
- dt_bias_grad: float32 [24], replicated
- a_log_grad: float32 [24], replicated
- skip_grad: float32 [24], replicated
- gate_gain_grad: float32 [1536], replicated
- output_rms: float32 [1], replicated
- mixer_rms: float32 [1], replicated
Inputs may be any that keep to these rules, and one draw needn't show every extreme that they name: Within each sequence segment_ids never fall, are 0 at the first position and rise by one exactly where doc_starts is 1; every sequence holds exactly 8 documents. `doc_starts`: 1 at the first position of every sequence; exactly 8 ones in every sequence.
All inputs are finite; a program needn't handle non-finite values.
Results may differ from a plain program's by a relative error of at most 0.0066.
The roundings to bfloat16 on the way count: a program that leaves them out, or rounds other values in their place, can miss the bound.
Values may be sent and summed in bfloat16 or wider, within the bound.
A program may use at most 192 MiB of HBM per device.

v0:
```python
import jax
import jax.numpy as jnp
from jax import lax
from jax.sharding import PartitionSpec as P

epsilon = 1e-05
highest = lax.Precision.HIGHEST


def shifted(block, axis, distance):
    devices = range(lax.axis_size(axis))
    route = [(i - distance, i) for i in devices if i - distance in devices]
    return lax.ppermute(block, axis, route)


def entering(value, axis, join, neutral):
    place = lax.axis_index(axis)
    gathered = jax.tree.map(
        lambda a, kind: lax.all_gather(a.astype(kind), axis), value, (jnp.bfloat16, jnp.bfloat16)
    )
    state = jax.tree.map(lambda a, e: jnp.zeros_like(a) + jnp.asarray(e, a.dtype), value, neutral)

    def one(step, state):
        return join(
            state,
            jax.tree.map(
                lambda a, own: lax.dynamic_index_in_dim(a, step, 0, False).astype(own.dtype),
                gathered,
                value,
            ),
        )

    return lax.fori_loop(0, place, one, state)


def carried_in(value, axis, combine, identity):
    length, mine = (lax.axis_size(axis), lax.axis_index(axis))
    everything = jax.tree.map(lambda part: lax.all_gather(part, axis), value)
    start = jax.tree.map(
        lambda part, zero: jnp.broadcast_to(jnp.asarray(zero, part.dtype), part.shape),
        value,
        identity,
    )

    def step(k, before):
        at = length - 1 - k
        reached = at > mine
        new = combine(before, jax.tree.map(lambda part: part[at], everything))
        return jax.tree.map(lambda a, b: jnp.where(reached, a, b), new, before)

    return lax.fori_loop(0, length, step, start)


def pre_norm(values, gain_values):
    return (
        values
        * lax.rsqrt(jnp.mean(values * values, axis=-1, keepdims=True) + epsilon)
        * gain_values
    )


def compose(earlier, later):
    return (earlier[0] * later[0], later[0][:, :, None, None] * earlier[1] + later[1])


def local(
    tokens,
    cotangent,
    segment_ids,
    doc_starts,
    valid_mask,
    step_number,
    learn_rate,
    norm_gain,
    in_weight,
    conv_weight,
    conv_bias,
    dt_bias,
    a_log,
    skip_d,
    gate_gain,
    out_weight,
    in_momentum,
    out_momentum,
):
    seq_count, piece_size, model_width = tokens.shape
    head_count = dt_bias.shape[0]
    tap_count, channels = conv_weight.shape
    inner_width = gate_gain.shape[0]
    state_width = (channels - inner_width) // 2
    head_width = inner_width // head_count
    proj_width = in_weight.shape[1]
    row_count = seq_count * piece_size
    inputs = tokens.astype(jnp.float32)
    normed_in, back_pre = jax.vjp(pre_norm, inputs, norm_gain)
    normed_low = normed_in.astype(jnp.bfloat16).reshape(row_count, model_width)
    projected = jnp.dot(normed_low, in_weight, preferred_element_type=jnp.float32).reshape(
        seq_count, piece_size, proj_width
    )
    gate_in = projected[:, :, :inner_width]
    conv_in = projected[:, :, inner_width : inner_width + channels]
    dt_raw = projected[:, :, inner_width + channels :]
    seg_float = segment_ids.astype(jnp.float32)
    prev_rows, prev_seg = shifted(
        (conv_in[:, piece_size - tap_count + 1 :], seg_float[:, piece_size - tap_count + 1 :]),
        "seq",
        1,
    )
    padded = jnp.concatenate([prev_rows, conv_in], axis=1)
    seg_pad = jnp.concatenate([prev_seg, seg_float], axis=1)
    masks = [
        (seg_pad[:, k : k + piece_size] == seg_float).astype(jnp.float32)[:, :, None]
        for k in range(tap_count)
    ]

    def conv_part(padded_in, taps_in, bias_in, raw_in, dt_bias_in, a_log_in):
        summed = bias_in + jnp.zeros((seq_count, piece_size, channels), jnp.float32)
        for k in range(tap_count):
            summed = summed + padded_in[:, k : k + piece_size] * masks[k] * taps_in[k]
        activated = jax.nn.silu(summed)
        signal = activated[:, :, :inner_width].reshape(
            seq_count, piece_size, head_count, head_width
        )
        writer = activated[:, :, inner_width : inner_width + state_width]
        reader = activated[:, :, inner_width + state_width :]
        step_size = jax.nn.softplus(raw_in + dt_bias_in)
        return (signal, writer, reader, step_size, -jnp.exp(a_log_in) * step_size)

    (signal, writer, reader, step_size, log_decay), back_conv = jax.vjp(
        conv_part, padded, conv_weight, conv_bias, dt_raw, dt_bias, a_log
    )
    counter = jnp.cumsum(doc_starts, axis=1)
    positions = jnp.arange(piece_size)
    causal = positions[:, None] >= positions[None, :]
    same_doc = (counter[:, :, None] == counter[:, None, :]) & causal[None]
    first_doc = (counter == 0)[:, :, None]
    last_doc = (counter == counter[:, -1:])[:, :, None]
    untouched = (counter[:, -1] == 0)[:, None]

    def end_state(signal_in, writer_in, step_in, decay_in):
        cumulative = jnp.cumsum(decay_in, axis=1)
        final_log = cumulative[:, -1]
        keeping = jnp.where(untouched, jnp.exp(final_log), 0.0)
        tails = jnp.where(last_doc, jnp.exp(final_log[:, None] - cumulative), 0.0) * step_in
        fresh_state = jnp.einsum(
            "slh,slhp,sln->shpn", tails, signal_in, writer_in, precision=highest
        )
        return (keeping, fresh_state)

    def piece_out(signal_in, writer_in, reader_in, step_in, decay_in, incoming_in):
        cumulative = jnp.cumsum(decay_in, axis=1)
        by_head = jnp.transpose(cumulative, (0, 2, 1))
        gaps = by_head[:, :, :, None] - by_head[:, :, None, :]
        decays = jnp.exp(jnp.where(same_doc[:, None], gaps, -1e30))
        scores = jnp.einsum("stn,sun->stu", reader_in, writer_in, precision=highest)
        weighted = scores[:, None] * decays
        inner_part = jnp.einsum(
            "shtu,suhp->sthp", weighted, signal_in * step_in[..., None], precision=highest
        )
        entries = jnp.where(first_doc, jnp.exp(cumulative), 0.0)
        carried = (
            jnp.einsum("stn,shpn->sthp", reader_in, incoming_in, precision=highest)
            * entries[..., None]
        )
        return inner_part + carried

    (keeping, fresh_state), back_end = jax.vjp(end_state, signal, writer, step_size, log_decay)
    identity = (jnp.ones_like(keeping), jnp.zeros_like(fresh_state))
    _, incoming = entering((keeping, fresh_state), "seq", compose, identity)
    ssm_out, back_out = jax.vjp(piece_out, signal, writer, reader, step_size, log_decay, incoming)

    def gate_norm(ssm_in, signal_in, skip_in, gate_values, gain_values):
        mixer_in = (ssm_in + skip_in[:, None] * signal_in).reshape(
            seq_count, piece_size, inner_width
        )
        gated_out = mixer_in * jax.nn.silu(gate_values)
        return (
            gated_out
            * lax.rsqrt(jnp.mean(gated_out * gated_out, axis=-1, keepdims=True) + epsilon)
            * gain_values
        )

    gate_normed, back_gate = jax.vjp(gate_norm, ssm_out, signal, skip_d, gate_in, gate_gain)
    gate_low = gate_normed.astype(jnp.bfloat16).reshape(row_count, inner_width)
    mixed = jnp.dot(gate_low, out_weight, preferred_element_type=jnp.float32).reshape(
        seq_count, piece_size, model_width
    )
    block_out = inputs + mixed
    valid_float = valid_mask.astype(jnp.float32)
    out_square = jnp.sum(valid_float * jnp.sum(block_out * block_out, axis=-1))
    mix_square = jnp.sum(valid_float * jnp.sum(mixed * mixed, axis=-1))
    valid_count = jnp.sum(valid_float)
    out_grad = cotangent.astype(jnp.float32) * valid_float[:, :, None]
    out_low = out_grad.astype(jnp.bfloat16).reshape(row_count, model_width)
    gate_grad = lax.dot_general(
        out_low, out_weight, (((1,), (1,)), ((), ())), preferred_element_type=jnp.float32
    ).reshape(seq_count, piece_size, inner_width)
    ssm_grad, signal_grad_gate, skip_grad, gate_in_grad, gate_gain_grad = back_gate(gate_grad)
    signal_grad_out, writer_grad_out, reader_grad, step_grad_out, decay_grad_out, state_grad = (
        back_out(ssm_grad)
    )
    _, later_grad = carried_in((keeping, state_grad), "seq", compose, identity)
    keeping_grad = jnp.sum(later_grad * incoming, axis=(2, 3))
    signal_grad_end, writer_grad_end, step_grad_end, decay_grad_end = back_end(
        (keeping_grad, later_grad)
    )
    padded_grad, conv_weight_grad, conv_bias_grad, dt_raw_grad, dt_bias_grad, a_log_grad = (
        back_conv(
            (
                signal_grad_gate + signal_grad_out + signal_grad_end,
                writer_grad_out + writer_grad_end,
                reader_grad,
                step_grad_out + step_grad_end,
                decay_grad_out + decay_grad_end,
            )
        )
    )
    rim_grad = shifted(padded_grad[:, : tap_count - 1].astype(jnp.bfloat16), "seq", -1).astype(
        jnp.float32
    )
    conv_in_grad = padded_grad[:, tap_count - 1 :] + jnp.pad(
        rim_grad, ((0, 0), (piece_size - tap_count + 1, 0), (0, 0))
    )
    proj_grad = (
        jnp.concatenate([gate_in_grad, conv_in_grad, dt_raw_grad], axis=2)
        .astype(jnp.bfloat16)
        .reshape(row_count, proj_width)
    )
    normed_grad = lax.dot_general(
        proj_grad, in_weight, (((1,), (1,)), ((), ())), preferred_element_type=jnp.float32
    ).reshape(seq_count, piece_size, model_width)
    input_grad_pre, norm_gain_grad = back_pre(normed_grad)
    input_grad = (out_grad + input_grad_pre).astype(jnp.bfloat16)
    share_rows = model_width // lax.axis_size("seq")
    in_part = lax.dot_general(
        normed_low, proj_grad, (((0,), (0,)), ((), ())), preferred_element_type=jnp.float32
    )
    out_part = lax.dot_general(
        out_low, gate_low, (((0,), (0,)), ((), ())), preferred_element_type=jnp.float32
    )
    whole_grad = lax.psum(jnp.concatenate([in_part, out_part], axis=1), "dp")
    grad_share = lax.psum_scatter(whole_grad, "seq", scatter_dimension=0, tiled=True)
    step_float = step_number[0].astype(jnp.float32)
    rate_now = learn_rate[0] * step_float / (step_float + 16.0)
    new_in_momentum = 0.5 * in_momentum + grad_share[:, :proj_width]
    new_out_momentum = 0.5 * out_momentum + jnp.transpose(grad_share[:, proj_width:])
    first_row = lax.axis_index("seq") * share_rows
    own_in = lax.dynamic_slice_in_dim(in_weight, first_row, share_rows, 0).astype(jnp.float32)
    own_out = lax.dynamic_slice_in_dim(out_weight, first_row, share_rows, 1).astype(jnp.float32)
    new_in_part = (own_in - rate_now * new_in_momentum).astype(jnp.bfloat16)
    new_out_part = (own_out - rate_now * new_out_momentum).astype(jnp.bfloat16)
    new_in_weight, new_out_weight = (
        lax.all_gather(new_in_part, "seq", axis=0, tiled=True),
        lax.all_gather(new_out_part, "seq", axis=1, tiled=True),
    )
    (
        norm_gain_total,
        conv_weight_total,
        conv_bias_total,
        dt_bias_total,
        a_log_total,
        skip_total,
        gate_gain_total,
        out_square_total,
        mix_square_total,
        valid_total,
    ) = lax.psum(
        (
            norm_gain_grad,
            conv_weight_grad,
            conv_bias_grad,
            dt_bias_grad,
            a_log_grad,
            skip_grad,
            gate_gain_grad,
            out_square,
            mix_square,
            valid_count,
        ),
        ("dp", "seq"),
    )
    denominator = jnp.maximum(valid_total, 1.0) * model_width
    output_rms = jnp.sqrt(out_square_total / denominator).reshape(1)
    mixer_rms = jnp.sqrt(mix_square_total / denominator).reshape(1)
    return (
        block_out.astype(jnp.bfloat16),
        input_grad,
        new_in_weight,
        new_out_weight,
        new_in_momentum,
        new_out_momentum,
        norm_gain_total,
        conv_weight_total,
        conv_bias_total,
        dt_bias_total,
        a_log_total,
        skip_total,
        gate_gain_total,
        output_rms,
        mixer_rms,
    )


def solution(mesh):
    placed = (
        P("dp", "seq", None),
        P("dp", "seq", None),
        P("dp", "seq"),
        P("dp", "seq"),
        P("dp", "seq"),
        P(),
        P(),
        P(),
        P(),
        P(),
        P(),
        P(),
        P(),
        P(),
        P(),
        P(),
        P("seq", None),
        P(None, "seq"),
    )
    return jax.shard_map(
        local,
        mesh=mesh,
        in_specs=placed,
        out_specs=(
            P("dp", "seq", None),
            P("dp", "seq", None),
            P(),
            P(),
            P("seq", None),
            P(None, "seq"),
            P(),
            P(),
            P(),
            P(),
            P(),
            P(),
            P(),
            P(),
            P(),
        ),
        check_vma=False,
    )
```

profile of v0, /device:TPU:0, one launch (start us, length us, event | category | flops | bytes accessed | tf_op | source)
XLA Modules:
  0.0 885.2 jit_solution(818629642145929513)
XLA Ops:
  9.2 5.5 convolution_bitcast_fusion
  14.8 4.9 collective-permute-start
  19.9 3.5 collective-permute-start.1
  25.9 4.2 slice.132
  36.3 11.6 %fusion.26 = (f32[1,512,1792]{2,1,0:T(8,128)S(1)}, f32[1,512,1792]{2,1,0:T(8,128)}) fusion(f32[1792]{0:T(1024)S(1)} %get-tuple-element.401, f32[1,512,1792]{2,1,0:T(8,128)} %slice.132, f32[512]{0:T(512)S(1)} %bitcast.377, f32[1792]{0:T(1024)S(1)} %get-tuple-element.402, f32[512]{0:T(512)S(1)} %bitcast.374, f32[1,3,1792]{2,1,0:T(4,128)S(1)} %copy.241, ...), kind=kLoop, calls=%fused_computation.50 | loop fusion | flops 17432576 | bytes 11075584 | tf_op jit(solution)/shard_map/jvp(jit(silu))/mul | solution.py:120
  49.8 2.1 slice.142
  51.9 2.4 copy.242
  54.3 4.3 fusion.70
  65.2 2.9 mul.637
  68.0 3.5 copy.254
  71.5 9.9 %all_gather.26 = bf16[4,1,24]{2,1,0:T(2,128)(2,1)} all-gather(bf16[1,1,24]{2,1,0:T(2,128)(2,1)} %get-tuple-element.453), channel_id=1, replica_groups=mesh['dp'=8,'seq'=4] {'seq'}, dimensions={0}, use_global_device_ids=true | all-gather | bytes 240 | tf_op jit(solution)/shard_map/all_gather | solution.py:19
  84.5 3.0 fusion.111
  87.5 7.6 all-gather.11.cloned.1.call-done
  96.4 4.0 fusion.88
  100.5 29.3 %fusion.30 = f32[1,512,24,64]{1,3,2,0:T(8,128)} fusion(f32[1,512,24,64]{1,3,2,0:T(8,128)S(1)} %bitcast.337, f32[512,24,64]{0,2,1:T(8,128)S(1)} %fusion.88, f32[24]{0:T(128)S(1)} %copy-done.89, f32[512,24]{0,1:T(8,128)S(1)} %copy-done.35, f32[24,512]{1,0:T(8,128)S(1)} %copy-done.45, f32[512,512]{1,0:T(8,128)S(1)} %copy-done.27, ...), kind=kOutput, calls=%fused_computation.59 | convolution fusion | flops 4854644736 | bytes 14041184 | tf_op jit(solution)/shard_map/jvp(shtu,suhp->sthp)/dot_general | solution.py:157
  129.8 3.6 copy.252
  133.4 4.0 multiply_reduce_fusion.7
  137.4 2.3 fusion.31
  141.5 5.6 multiply_reduce_fusion.5
  148.8 2.2 mul.669
  151.0 12.4 %copy.255 = f32[1,512,1536]{1,2,0:T(8,128)} copy(f32[1,512,1536]{2,1,0:T(8,128)} %mul.669) | data formatting | bytes 6291456 | tf_op jit(solution)/shard_map/transpose(jvp())/mul | solution.py:162
  163.4 5.4 fusion.107
  168.9 17.8 %all_gather.29 = f32[4,1,24]{2,1,0:T(1,128)} all-gather(f32[1,1,24]{2,1,0:T(1,128)S(1)} %copy-done.87), channel_id=1, replica_groups=mesh['dp'=8,'seq'=4] {'seq'}, dimensions={0}, use_global_device_ids=true | all-gather | bytes 480 | tf_op jit(solution)/shard_map/all_gather | solution.py:38
  186.7 3.5 copy.256
  190.2 3.7 multiply_reduce_fusion.6
  194.8 33.7 %fusion.7 = (f32[24,512]{1,0:T(8,128)}, f32[24,512]{1,0:T(8,128)S(1)}, f32[512,512]{1,0:T(8,128)}) fusion(f32[24,512]{1,0:T(8,128)} %bitcast_add_fusion.6, f32[512,512]{1,0:T(8,128)} %fusion.111, pred[512,512]{1,0:T(8,128)(4,1)} %fusion.81, f32[24,64,512]{2,1,0:T(8,128)} %bitcast.346, f32[512,24,64]{0,2,1:T(8,128)S(1)} %bitcast.339, f32[512,24]{0,1:T(8,128)} %copy.243), kind=kOutput, calls=%fused_computation.12 | convolution fusion | flops 4888961024 | bytes 8847360 | tf_op jit(solution)/shard_map/transpose(jvp(shtu,suhp->sthp))/dot_general | solution.py:157
  230.9 3.9 convolution_bitcast_fusion.1
  234.9 7.1 convolution_bitcast_fusion.2
  242.0 2.6 fusion.79
  244.7 3.9 fusion.91
  248.6 22.4 %fusion.2 = f32[24,64,512]{2,1,0:T(8,128)} fusion(f32[24,64,512]{2,1,0:T(8,128)S(1)} %bitcast.347, f32[24,512]{1,0:T(8,128)S(1)} %copy-done.46, f32[512,512]{1,0:T(8,128)S(1)} %copy-done.28, pred[512,512]{1,0:T(8,128)(4,1)S(1)} %copy-done.33), kind=kOutput, calls=%fused_computation.9 | convolution fusion | flops 4850712576 | bytes 7651328 | tf_op jit(solution)/shard_map/transpose(jvp(shtu,suhp->sthp))/dot_general | solution.py:157
  271.0 12.0 %while.29 = (s32[]{:T(128)}, f32[1,24,64,128]{3,2,1,0:T(8,128)}, s32[]{:T(128)}, f32[4,1,24]{2,1,0:T(1,128)}, f32[4,1,24,64,128]{4,3,2,1,0:T(8,128)}, /*index=5*/s32[]{:T(128)}, s32[]{:T(128)}, s32[]{:T(128)}, s32[]{:T(128)}) while((s32[]{:T(128)}, f32[1,24,64,128]{3,2,1,0:T(8,128)}, s32[]{:T(128)}, f32[4,1,24]{2,1,0:T(1,128)}, ...), condition=%wide.region_11.12_spmd.clone, body=%wide.region_10.11_spmd.clone.sunk | while | flops 786440 | bytes 2359751 | solution.py:51
  271.5 2.2 fusion.159
  274.3 2.4 fusion.159
  277.4 2.4 fusion.159
  280.4 2.4 fusion.159
  283.0 4.1 fusion.34
  288.0 5.8 fusion.76
  293.8 4.2 fusion.33
  298.0 2.4 copy.260
  300.5 11.2 %multiply_reduce_fusion.3 = (f32[1792]{0:T(1024)}, f32[1792]{0:T(1024)S(1)}, f32[1792]{0:T(1024)}, f32[1792]{0:T(1024)S(1)}, f32[1792]{0:T(1024)}, /*index=5*/f32[1,512,1792]{2,1,0:T(8,128)S(1)}) fusion(f32[1,512,1792]{2,1,0:T(8,128)} %slice.132, f32[1,3,1792]{2,1,0:T(4,128)S(1)} %copy.241, f32[512]{0:T(512)S(1)} %bitcast.375, f32[512]{0:T(512)S(1)} %bitcast.369, ...), kind=kLoop, calls=%fused_computation.43 | loop fusion | flops 24763648 | bytes 18415616 | tf_op jit(solution)/shard_map/transpose(jvp())/reduce_sum | solution.py:119
  314.5 1.9 copy-done.12
  319.6 5.0 reduce-window.36
  324.8 5.0 reduce-window.34
  331.9 2.5 fusion.48
  334.5 3.1 fusion.68
  337.7 5.8 pad_maximum_fusion
  343.4 15.2 %copy.289 = f32[768,4888]{1,0:T(8,128)} copy(f32[768,4888]{0,1:T(8,128)} %pad_maximum_fusion) | data formatting | bytes 30031872
  358.6 256.6 %reduce-scatter.4.cloned.1.call-done = f32[192,4888]{1,0:T(8,128)} async-done(((f32[768,4888]{1,0:T(8,128)}), f32[192,4888]{1,0:T(8,128)}) %reduce-scatter.4.cloned.1.call-update) | async-done | bytes 3754000
  615.2 5.7 copy.290
  622.9 89.6 %all-reduce.16.cloned.1.call-done = f32[192,4888]{0,1:T(8,128)} async-done(((f32[192,4888]{0,1:T(8,128)}), f32[192,4888]{0,1:T(8,128)}) %all-reduce.16.cloned.1.call-update) | async-done | bytes 3754000 | tf_op jit(solution)/shard_map/psum | solution.py:241
  712.5 3.5 subtract_convert_fusion.1
  717.1 3.6 copy.270
  720.7 6.4 subtract_convert_fusion
  727.1 3.8 copy.272
  731.3 3.3 multiply_reduce_fusion.8
  734.9 7.1 fusion.50
  742.6 42.8 %all-reduce.13 = (f32[768]{0:T(1024)}, f32[4,1792]{1,0:T(4,128)}, f32[1792]{0:T(1024)}, f32[24]{0:T(128)}, f32[24]{0:T(128)}, /*index=5*/f32[24]{0:T(128)}, f32[1536]{0:T(1024)}, f32[]{:T(128)}, f32[]{:T(128)}, f32[]{:T(128)}) all-reduce(f32[768]{0:T(1024)S(1)} %get-tuple-element.396, ...), channel_id=1, replica_groups=mesh['dp'=8,'seq'=4] {'dp','seq'}, use_global_device_ids=true, to_apply=%region_26.27 | all-reduce | flops 11339 | bytes 90712 | tf_op jit(solution)/shard_map/psum | solution.py:267
  787.5 3.3 fusion.52
  790.8 2.9 copy.277
  793.7 2.9 copy.278
  796.5 4.3 copy.276
  800.8 66.9 %all-gather.7.cloned.1.call-done = bf16[768,3352]{1,0:T(8,128)(2,1)} async-done(((bf16[192,3352]{1,0:T(8,128)(2,1)}), bf16[768,3352]{1,0:T(8,128)(2,1)}) %all-gather.7.cloned.1.call-update) | async-done | bytes 5148688 | tf_op jit(solution)/shard_map/all_gather | solution.py:253
  867.7 8.0 copy.275
  (290 shorter events, 42.9 us)
Async XLA Ops:
  7.2 88.0 %all-gather.11.cloned.1.call-start = ((), (), s32[]{:S(2)}) async-start(), calls=%async_computation.3 | async-start | bytes 1966080 | tf_op jit(solution)/shard_map/all_gather | solution.py:19
  9.2 5.6 copy-start.69
  9.2 10.6 %copy-start.72 = (s32[1,512]{1,0:T(1,128)S(1)}, s32[1,512]{1,0:T(1,128)}, u32[]{:S(2)}) copy-start(s32[1,512]{1,0:T(1,128)} %param.24) | copy-start | bytes 6148
  9.2 14.2 %copy-start.91 = (f32[24]{0:T(128)S(1)}, f32[24]{0:T(128)}, u32[]{:S(2)}) copy-start(f32[24]{0:T(128)} %param.34) | copy-start | bytes 292
  9.2 14.2 %copy-start.75 = (f32[24]{0:T(128)S(1)}, f32[24]{0:T(128)}, u32[]{:S(2)}) copy-start(f32[24]{0:T(128)} %param.33) | copy-start | bytes 292
  14.8 8.6 copy-start.4
  14.8 21.5 %collective-permute-start = (f32[1,3,1792]{2,0,1:T(1,128)S(1)}, f32[1,3,1792]{2,0,1:T(1,128)S(1)}, u32[]{:S(2)}, u32[]{:S(2)}) collective-permute-start(f32[1,3,1792]{2,0,1:T(1,128)S(1)} %copy.240), channel_id=1, source_target_pairs={{0,1},{1,2},{2,3},{4,5},{5,6},{6,7},{8,9},{9,10},{10,11},{12,13},{... | collective-permute-start | bytes 64520 | tf_op jit(solution)/shard_map/ppermute | solution.py:13
  19.9 16.3 %collective-permute-start.1 = (f32[1,3]{1,0:T(1,128)S(1)}, f32[1,3]{1,0:T(1,128)S(1)}, u32[]{:S(2)}, u32[]{:S(2)}) collective-permute-start(f32[1,3]{1,0:T(1,128)S(1)} %slice.135), channel_id=1, source_target_pairs={{0,1},{1,2},{2,3},{4,5},{5,6},{6,7},{8,9},{9,10},{10,11},{12,13},{... | collective-permute-start | bytes 44 | tf_op jit(solution)/shard_map/ppermute | solution.py:13
  25.8 4.3 copy-start.88
  25.8 10.2 %copy-start.63 = (f32[4,1792]{1,0:T(4,128)S(1)}, f32[4,1792]{1,0:T(4,128)}, u32[]{:S(2)}) copy-start(f32[4,1792]{1,0:T(4,128)} %param.31) | copy-start | bytes 86020
  25.8 10.5 %copy-start.74 = (f32[1792]{0:T(1024)S(1)}, f32[1792]{0:T(1024)}, u32[]{:S(2)}) copy-start(f32[1792]{0:T(1024)} %param.32) | copy-start | bytes 21508
  30.0 17.9 %copy-start.57 = (f32[1,512]{1,0:T(1,128)}, f32[1,512]{1,0:T(1,128)S(1)}, u32[]{:S(2)}) copy-start(f32[1,512]{1,0:T(1,128)S(1)} %compare_convert_fusion) | copy-start | bytes 6148
  30.8 17.1 %copy-start.62 = (s32[512]{0:T(512)}, s32[512]{0:T(512)S(1)}, u32[]{:S(2)}) copy-start(s32[512]{0:T(512)S(1)} %get-tuple-element.452) | copy-start | bytes 6148
  36.1 11.8 %copy-start.41 = (f32[1792]{0:T(1024)}, f32[1792]{0:T(1024)S(1)}, u32[]{:S(2)}) copy-start(f32[1792]{0:T(1024)S(1)} %get-tuple-element.401) | copy-start | bytes 21508
  36.2 11.8 %copy-start.43 = (f32[1792]{0:T(1024)}, f32[1792]{0:T(1024)S(1)}, u32[]{:S(2)}) copy-start(f32[1792]{0:T(1024)S(1)} %get-tuple-element.402) | copy-start | bytes 21508
  36.3 11.7 %copy-start.51 = (f32[1,512]{1,0:T(1,128)}, f32[1,512]{1,0:T(1,128)S(1)}, u32[]{:S(2)}) copy-start(f32[1,512]{1,0:T(1,128)S(1)} %get-tuple-element.470) | copy-start | bytes 6148
  36.3 11.7 %copy-start.53 = (f32[1,512]{1,0:T(1,128)}, f32[1,512]{1,0:T(1,128)S(1)}, u32[]{:S(2)}) copy-start(f32[1,512]{1,0:T(1,128)S(1)} %get-tuple-element.471) | copy-start | bytes 6148
  36.3 11.7 %copy-start.55 = (f32[1,512]{1,0:T(1,128)}, f32[1,512]{1,0:T(1,128)S(1)}, u32[]{:S(2)}) copy-start(f32[1,512]{1,0:T(1,128)S(1)} %get-tuple-element.472) | copy-start | bytes 6148
  58.7 212.3 %all-gather.13.cloned.1.call-start = ((), (), s32[]{:S(2)}) async-start(), calls=%async_computation.4 | async-start | bytes 3932160 | tf_op jit(solution)/shard_map/all_gather | solution.py:38
  100.4 29.4 %copy-start.14 = (f32[512,24,64]{0,2,1:T(8,128)}, f32[512,24,64]{0,2,1:T(8,128)S(1)}, u32[]{:S(2)}) copy-start(f32[512,24,64]{0,2,1:T(8,128)S(1)} %fusion.88) | copy-start | bytes 9437188
  137.4 4.1 copy-start.5
  141.5 7.3 copy-start.15
  163.4 5.5 copy-start.87
  168.8 446.4 %reduce-scatter.4.cloned.1.call-start = ((), (), s32[]{:S(2)}) async-start(), calls=%async_computation.6 | async-start | bytes 19169280
  230.9 11.1 %copy-start.18 = (f32[512,512]{1,0:T(8,128)S(1)}, f32[512,512]{1,0:T(8,128)}, u32[]{:S(2)}) copy-start(f32[512,512]{1,0:T(8,128)} %get-tuple-element.388) | copy-start | bytes 3145732
  230.9 13.7 %copy-start.7 = (f32[1,512,1536]{2,1,0:T(8,128)S(1)}, f32[1,512,1536]{2,1,0:T(8,128)}, u32[]{:S(2)}) copy-start(f32[1,512,1536]{2,1,0:T(8,128)} %copy-done.6) | copy-start | bytes 9437188
  230.9 13.7 %copy-start.17 = (bf16[1,512,768]{2,1,0:T(8,128)(2,1)S(1)}, bf16[1,512,768]{2,1,0:T(8,128)(2,1)}, u32[]{:S(2)}) copy-start(bf16[1,512,768]{2,1,0:T(8,128)(2,1)} %param.23) | copy-start | bytes 2359300
  230.9 13.7 %copy-start.48 = (f32[1536]{0:T(1024)S(1)}, f32[1536]{0:T(1024)}, u32[]{:S(2)}) copy-start(f32[1536]{0:T(1024)} %param.36) | copy-start | bytes 18436
  230.9 13.7 %copy-start.65 = (f32[512]{0:T(512)S(1)}, f32[512]{0:T(512)}, u32[]{:S(2)}) copy-start(f32[512]{0:T(512)} %copy-done.64) | copy-start | bytes 6148
  283.0 4.2 copy-start
  283.0 4.2 copy-start.1
  283.0 5.0 copy-start.29
  283.0 10.8 %copy-start.21 = (f32[24,64,512]{2,1,0:T(8,128)S(1)}, f32[24,64,512]{2,1,0:T(8,128)}, u32[]{:S(2)}) copy-start(f32[24,64,512]{2,1,0:T(8,128)} %fusion.2) | copy-start | bytes 9437188
  287.2 6.6 copy-start.11
  287.2 6.6 copy-start.37
  287.2 6.6 copy-start.90
  300.5 11.2 %copy-start.42 = (f32[1792]{0:T(1024)S(1)}, f32[1792]{0:T(1024)}, u32[]{:S(2)}) copy-start(f32[1792]{0:T(1024)} %copy-done.41) | copy-start | bytes 21508
  300.5 11.2 %copy-start.44 = (f32[1792]{0:T(1024)S(1)}, f32[1792]{0:T(1024)}, u32[]{:S(2)}) copy-start(f32[1792]{0:T(1024)} %copy-done.43) | copy-start | bytes 21508
  313.3 4.7 copy-start.30
  313.4 4.7 copy-start.31
  313.4 4.7 copy-start.76
  313.4 4.7 copy-start.78
  313.4 4.7 copy-start.80
  313.4 4.7 copy-start.82
  313.4 6.0 copy-start.86
  316.4 13.7 %copy-start.38 = (f32[512,24]{0,1:T(8,128)S(1)}, f32[512,24]{0,1:T(8,128)}, u32[]{:S(2)}) copy-start(f32[512,24]{0,1:T(8,128)} %get-tuple-element.466) | copy-start | bytes 147460
  316.4 13.9 %copy-start.85 = (f32[24]{0:T(128)S(1)}, f32[24]{0:T(128)}, u32[]{:S(2)}) copy-start(f32[24]{0:T(128)} %copy-done.84) | copy-start | bytes 292
  316.5 15.4 %collective-permute-start.2 = (bf16[1,3,1792]{2,1,0:T(4,128)(2,1)S(1)}, bf16[1,3,1792]{2,1,0:T(4,128)(2,1)S(1)}, u32[]{:S(2)}, u32[]{:S(2)}) collective-permute-start(bf16[1,3,1792]{2,1,0:T(4,128)(2,1)S(1)} %slice.284), channel_id=1, source_target_pairs={{1,0},{2,1},{3,2},{5,4},{6,5},{7,6},{9,8},{10,9},{11,10},{13,12},{... | collective-permute-start | bytes 32264 | tf_op jit(solution)/shard_map/ppermute | solution.py:13
  330.3 4.1 copy-start.19
  330.3 4.1 copy-start.24
  330.4 4.1 copy-start.70
  330.4 4.1 copy-start.83
  331.9 5.7 copy-start.39
  331.9 5.7 slice-start
  358.6 353.9 %all-reduce.16.cloned.1.call-start = ((), (), s32[]{:S(2)}) async-start(), calls=%async_computation.5 | async-start | bytes 10010624 | tf_op jit(solution)/shard_map/psum | solution.py:241
  621.0 175.6 %all-gather.9.cloned.1.call-start = ((), (), s32[]{:S(2)}) async-start(), calls=%async_computation.2 | async-start | bytes 2949120 | tf_op jit(solution)/shard_map/all_gather | solution.py:254
  717.1 150.7 %all-gather.7.cloned.1.call-start = ((), (), s32[]{:S(2)}) async-start(), calls=%async_computation.1 | async-start | bytes 6635520 | tf_op jit(solution)/shard_map/all_gather | solution.py:253
  727.1 4.1 copy-start.8
  727.1 4.1 copy-start.49
  727.1 4.1 copy-start.66
  734.8 7.2 copy-start.73
  734.8 7.8 copy-start.71
  734.9 52.6 %copy-start.68 = (f32[512]{0:T(512)S(1)}, f32[512]{0:T(512)}, u32[]{:S(2)}) copy-start(f32[512]{0:T(512)} %copy-done.67) | copy-start | bytes 6148
  742.0 48.8 %copy-start.13 = (f32[192,3352]{0,1:T(8,128)S(1)}, f32[192,3352]{0,1:T(8,128)}, u32[]{:S(2)}) copy-start(f32[192,3352]{0,1:T(8,128)} %get-tuple-element.444) | copy-start | bytes 7723012
  (40 other events, 122.4 us)
Sparse Core Ops, SparseCore 0:
  58.8 36.3 all-gather.10
  169.0 70.9 all-gather.12
  358.7 256.4 reduce-scatter.3
  621.1 91.3 all-reduce.15
  717.2 50.9 all-gather.8
  769.7 98.0 all-gather.6
where the time goes:
time: 895 us; the launch traced here: 885 us
  waiting for transfers between devices  421 us (47%)
  matrix products  151 us (17%)
  local copies, waits for them, and re-layouts  108 us (12%)
  other arithmetic  101 us (11%)
  blocking collectives  70.5 us (8%)
  between operations  23.1 us (3%)
  starting transfers between devices  10.1 us (1%)
    unnamed x7, waiting for transfers between devices  257 us
    psum x1, waiting for transfers between devices, local(): whole_grad = lax.psum(jnp.concatenate([in_part, out_part], axis=1), 'dp')  89.6 us
    dot_general x3, matrix products, piece_out(): jnp.einsum('shtu,suhp->sthp', weighted, signal_in * step_in[..., None], p...  85.3 us
    all_gather x1, waiting for transfers between devices, local(): lax.all_gather(new_in_part, 'seq', axis=0, tiled=True)  66.9 us
    unnamed x198, local copies, waits for them, and re-layouts  51 us
    psum x1, blocking collectives, local(): lax.psum((norm_gain_grad, conv_weight_grad, conv_bias_grad, dt_bias_grad,...  42.8 us
    mul x4, local copies, waits for them, and re-layouts, piece_out(): jnp.einsum('stn,shpn->sthp', reader_in, incoming_in, precision=highest)  20.4 us
  transfers between devices with their start and end apart: 9, of which 4 were waited for; matrix products, arithmetic and copies ran while one was open for 19% of the time, Pallas kernels for 0%

commit v1 on v0

--- a/solution.py
+++ b/solution.py
@@ -5,6 +5,27 @@
 
 epsilon = 1e-05
 highest = lax.Precision.HIGHEST
+
+
+def ring_gather(shard, axis, dim):
+    devices, position, width = (lax.axis_size(axis), lax.axis_index(axis), shard.shape[dim])
+    ahead = [(i, (i + 1) % devices) for i in range(devices)]
+    left = [(i, (i - 1) % devices) for i in range(devices)]
+    out = jnp.zeros((*shard.shape[:dim], devices * width, *shard.shape[dim + 1 :]), shard.dtype)
+    out = lax.dynamic_update_slice_in_dim(out, shard, position * width, axis=dim)
+    from_left = from_right = shard
+    half = devices // 2
+    for lap in range(1, half + 1):
+        from_left = lax.ppermute(from_left, axis, ahead)
+        out = lax.dynamic_update_slice_in_dim(
+            out, from_left, (position - lap) % devices * width, axis=dim
+        )
+        if lap < devices - half:
+            from_right = lax.ppermute(from_right, axis, left)
+            out = lax.dynamic_update_slice_in_dim(
+                out, from_right, (position + lap) % devices * width, axis=dim
+            )
+    return out
 
 
 def shifted(block, axis, distance):
@@ -250,7 +271,7 @@
     new_in_part = (own_in - rate_now * new_in_momentum).astype(jnp.bfloat16)
     new_out_part = (own_out - rate_now * new_out_momentum).astype(jnp.bfloat16)
     new_in_weight, new_out_weight = (
-        lax.all_gather(new_in_part, "seq", axis=0, tiled=True),
+        ring_gather(new_in_part, "seq", 0),
         lax.all_gather(new_out_part, "seq", axis=1, tiled=True),
     )
     (

time: 895 us -> 989 us (1.11)
  local copies, waits for them, and re-layouts: 108 us -> 182 us
  starting transfers between devices: 10.1 us -> 28.9 us
  blocking collectives: 70.5 us -> 87.3 us
  waiting for transfers between devices: 421 us -> 405 us
    dynamic_update_slice x0 -> x4, local copies, waits for them, and re-layouts: none -> 69.4 us  [the longest x2 34.1 us: ring_gather(): lax.dynamic_update_slice_in_dim(out, from_left, (position - lap) % device...]
    all_gather x1 -> x0, waiting for transfers between devices: 66.9 us -> none  [local(): lax.all_gather(new_in_part, 'seq', axis=0, tiled=True)]
    ppermute x0 -> x3, waiting for transfers between devices: none -> 54.8 us  [the longest x2 54.8 us: ring_gather(): from_left = lax.ppermute(from_left, axis, ahead)]
    ppermute x0 -> x3, starting transfers between devices: none -> 19 us  [the longest x2 16.7 us: ring_gather(): from_left = lax.ppermute(from_left, axis, ahead)]
    psum x1, blocking collectives: 42.8 us -> 60.3 us  [local(): lax.psum((norm_gain_grad, conv_weight_grad, conv_bias_grad, dt_bias_grad,...]
    unnamed x198 -> x209, local copies, waits for them, and re-layouts: 51 us -> 44.7 us
    unnamed x7 -> x6, waiting for transfers between devices: 257 us -> 257 us
  transfers between devices with their start and end apart: 9 -> 11, of which waited for: 4 -> 4; matrix products, arithmetic and copies ran while one was open for 19% -> 25% of each run, Pallas kernels for 0% -> 0%
where the time goes in v1:
time: 989 us; the launch traced here: 977 us
  waiting for transfers between devices  405 us (41%)
  local copies, waits for them, and re-layouts  182 us (18%)
  matrix products  151 us (15%)
  other arithmetic  100 us (10%)
  blocking collectives  87.3 us (9%)
  starting transfers between devices  28.9 us (3%)
  between operations  22.9 us (2%)
    unnamed x6, waiting for transfers between devices  257 us
    dot_general x3, matrix products, piece_out(): jnp.einsum('shtu,suhp->sthp', weighted, signal_in * step_in[..., None], p...  85.3 us
    psum x1, waiting for transfers between devices, local(): whole_grad = lax.psum(jnp.concatenate([in_part, out_part], axis=1), 'dp')  84.8 us
    psum x1, blocking collectives, local(): lax.psum((norm_gain_grad, conv_weight_grad, conv_bias_grad, dt_bias_grad,...  60.3 us
    ppermute x2, waiting for transfers between devices, ring_gather(): from_left = lax.ppermute(from_left, axis, ahead)  54.8 us
    unnamed x209, local copies, waits for them, and re-layouts  44.7 us
    dynamic_update_slice x2, local copies, waits for them, and re-layouts, ring_gather(): lax.dynamic_update_slice_in_dim(out, from_left, (position - lap) % device...  34.1 us
    mul x4, local copies, waits for them, and re-layouts, piece_out(): jnp.einsum('stn,shpn->sthp', reader_in, incoming_in, precision=highest)  20.4 us
  transfers between devices with their start and end apart: 11, of which 4 were waited for; matrix products, arithmetic and copies ran while one was open for 25% of the time, Pallas kernels for 0%

profile of v1, /device:TPU:0, one launch (start us, length us, event | category | flops | bytes accessed | tf_op | source)
XLA Modules:
  0.0 977.2 jit_solution(7025139243212119503)
XLA Ops:
  9.2 5.5 convolution_bitcast_fusion
  14.8 4.9 collective-permute-start
  19.9 3.5 collective-permute-start.1
  25.9 4.2 slice.132
  36.4 11.4 %fusion.26 = (f32[1,512,1792]{2,1,0:T(8,128)S(1)}, f32[1,512,1792]{2,1,0:T(8,128)}) fusion(f32[1792]{0:T(1024)S(1)} %get-tuple-element.401, f32[1,512,1792]{2,1,0:T(8,128)} %slice.132, f32[512]{0:T(512)S(1)} %bitcast.377, f32[1792]{0:T(1024)S(1)} %get-tuple-element.402, f32[512]{0:T(512)S(1)} %bitcast.374, f32[1,3,1792]{2,1,0:T(4,128)S(1)} %copy.253, ...), kind=kLoop, calls=%fused_computation.50 | loop fusion | flops 17432576 | bytes 11075584 | tf_op jit(solution)/shard_map/jvp(jit(silu))/mul | solution.py:141
  54.1 4.3 fusion.70
  64.9 2.9 mul.647
  67.8 3.5 copy.266
  71.3 9.2 all_gather.23
  83.6 3.0 fusion.111
  86.6 8.3 all-gather.8.cloned.1.call-done
  96.2 4.0 fusion.88
  100.3 29.3 %fusion.30 = f32[1,512,24,64]{1,3,2,0:T(8,128)} fusion(f32[1,512,24,64]{1,3,2,0:T(8,128)S(1)} %bitcast.337, f32[512,24,64]{0,2,1:T(8,128)S(1)} %fusion.88, f32[24]{0:T(128)S(1)} %copy-done.94, f32[512,24]{0,1:T(8,128)S(1)} %copy-done.38, f32[24,512]{1,0:T(8,128)S(1)} %copy-done.46, f32[512,512]{1,0:T(8,128)S(1)} %copy-done.30, ...), kind=kOutput, calls=%fused_computation.59 | convolution fusion | flops 4854644736 | bytes 14041184 | tf_op jit(solution)/shard_map/jvp(shtu,suhp->sthp)/dot_general | solution.py:178
  129.5 3.6 copy.264
  133.1 4.0 multiply_reduce_fusion.7
  141.2 5.6 multiply_reduce_fusion.5
  150.7 12.4 %copy.267 = f32[1,512,1536]{1,2,0:T(8,128)} copy(f32[1,512,1536]{2,1,0:T(8,128)} %mul.679) | data formatting | bytes 6291456 | tf_op jit(solution)/shard_map/transpose(jvp())/mul | solution.py:183
  163.1 5.4 fusion.107
  168.6 17.8 %all_gather.26 = f32[4,1,24]{2,1,0:T(1,128)} all-gather(f32[1,1,24]{2,1,0:T(1,128)S(1)} %copy-done.92), channel_id=1, replica_groups=mesh['dp'=8,'seq'=4] {'seq'}, dimensions={0}, use_global_device_ids=true | all-gather | bytes 480 | tf_op jit(solution)/shard_map/all_gather | solution.py:59
  186.4 3.5 copy.268
  189.9 3.7 multiply_reduce_fusion.6
  194.5 33.6 %fusion.7 = (f32[24,512]{1,0:T(8,128)}, f32[24,512]{1,0:T(8,128)S(1)}, f32[512,512]{1,0:T(8,128)}) fusion(f32[24,512]{1,0:T(8,128)} %bitcast_add_fusion.6, f32[512,512]{1,0:T(8,128)} %fusion.111, pred[512,512]{1,0:T(8,128)(4,1)} %fusion.81, f32[24,64,512]{2,1,0:T(8,128)} %bitcast.346, f32[512,24,64]{0,2,1:T(8,128)S(1)} %bitcast.339, f32[512,24]{0,1:T(8,128)} %copy.255), kind=kOutput, calls=%fused_computation.12 | convolution fusion | flops 4888961024 | bytes 8847360 | tf_op jit(solution)/shard_map/transpose(jvp(shtu,suhp->sthp))/dot_general | solution.py:178
  230.6 3.9 convolution_bitcast_fusion.1
  234.5 7.1 convolution_bitcast_fusion.2
  241.7 2.6 fusion.79
  244.4 3.9 fusion.91
  248.3 22.4 %fusion.2 = f32[24,64,512]{2,1,0:T(8,128)} fusion(f32[24,64,512]{2,1,0:T(8,128)S(1)} %bitcast.347, f32[24,512]{1,0:T(8,128)S(1)} %copy-done.47, f32[512,512]{1,0:T(8,128)S(1)} %copy-done.31, pred[512,512]{1,0:T(8,128)(4,1)S(1)} %copy-done.36), kind=kOutput, calls=%fused_computation.9 | convolution fusion | flops 4850712576 | bytes 7651328 | tf_op jit(solution)/shard_map/transpose(jvp(shtu,suhp->sthp))/dot_general | solution.py:178
  270.7 12.0 %while.29 = (s32[]{:T(128)}, f32[1,24,64,128]{3,2,1,0:T(8,128)}, s32[]{:T(128)}, f32[4,1,24]{2,1,0:T(1,128)}, f32[4,1,24,64,128]{4,3,2,1,0:T(8,128)}, /*index=5*/s32[]{:T(128)}, s32[]{:T(128)}, s32[]{:T(128)}, s32[]{:T(128)}) while((s32[]{:T(128)}, f32[1,24,64,128]{3,2,1,0:T(8,128)}, s32[]{:T(128)}, f32[4,1,24]{2,1,0:T(1,128)}, ...), condition=%wide.region_11.12_spmd.clone, body=%wide.region_10.11_spmd.clone.sunk | while | flops 786440 | bytes 2359751 | solution.py:72
  274.0 2.4 fusion.159
  277.0 2.4 fusion.159
  280.1 2.4 fusion.159
  282.7 4.1 fusion.34
  287.7 5.8 fusion.76
  293.5 4.2 fusion.33
  297.7 2.4 copy.272
  300.2 10.9 %multiply_reduce_fusion.3 = (f32[1792]{0:T(1024)}, f32[1792]{0:T(1024)}, f32[1792]{0:T(1024)}, f32[1792]{0:T(1024)}, f32[1792]{0:T(1024)}, /*index=5*/f32[1,512,1792]{2,1,0:T(8,128)S(1)}) fusion(f32[1,512,1792]{2,1,0:T(8,128)} %slice.132, f32[1,3,1792]{2,1,0:T(4,128)S(1)} %copy.253, f32[512]{0:T(512)S(1)} %bitcast.375, f32[512]{0:T(512)S(1)} %bitcast.369, ...), kind=kLoop, calls=%fused_computation.43 | loop fusion | flops 24763648 | bytes 18415616 | tf_op jit(solution)/shard_map/transpose(jvp())/reduce_sum | solution.py:140
  318.8 5.0 reduce-window.36
  324.0 5.0 reduce-window.34
  331.6 2.5 fusion.48
  334.2 3.1 fusion.68
  337.4 5.8 pad_maximum_fusion
  343.1 15.2 %copy.304 = f32[768,4888]{1,0:T(8,128)} copy(f32[768,4888]{0,1:T(8,128)} %pad_maximum_fusion) | data formatting | bytes 30031872
  358.4 256.6 %reduce-scatter.4.cloned.1.call-done = f32[192,4888]{1,0:T(8,128)} async-done(((f32[768,4888]{1,0:T(8,128)}), f32[192,4888]{1,0:T(8,128)}) %reduce-scatter.4.cloned.1.call-update) | async-done | bytes 3754000
  615.0 5.7 copy.305
  622.5 3.2 copy.282
  627.4 84.8 %all-reduce.16.cloned.1.call-done = f32[192,4888]{0,1:T(8,128)} async-done(((f32[192,4888]{0,1:T(8,128)}), f32[192,4888]{0,1:T(8,128)}) %all-reduce.16.cloned.1.call-update) | async-done | bytes 3754000 | tf_op jit(solution)/shard_map/psum | solution.py:262
  712.2 3.5 subtract_convert_fusion.1
  716.9 7.5 subtract_convert_fusion
  724.4 3.7 copy.284
  730.0 3.4 multiply_reduce_fusion.8
  735.8 54.8 %collective-permute-done.3 = bf16[192,3352]{1,0:T(8,128)(2,1)} collective-permute-done((bf16[192,3352]{1,0:T(8,128)(2,1)}, bf16[192,3352]{1,0:T(8,128)(2,1)}, u32[]{:S(2)}, u32[]{:S(2)}) %collective-permute-start.3) | collective-permute-done | bytes 1287200 | tf_op jit(solution)/shard_map/ppermute | solution.py:19
  790.6 15.2 %collective-permute-start.5 = (bf16[192,3352]{1,0:T(8,128)(2,1)}, bf16[192,3352]{1,0:T(8,128)(2,1)}, u32[]{:S(2)}, u32[]{:S(2)}) collective-permute-start(bf16[192,3352]{1,0:T(8,128)(2,1)} %collective-permute-done.3), channel_id=1, source_target_pairs={{0,1},{1,2},{2,3},{3,0},{4,5},{5,6},{6,7},{7,4},{8,9},{9,10},{10,1... | collective-permute-start | bytes 3861512 | tf_op jit(solution)/shard_map/ppermute | solution.py:19
  805.9 6.7 fusion.50
  813.2 60.3 %all-reduce.13 = (f32[768]{0:T(1024)}, f32[4,1792]{1,0:T(4,128)}, f32[1792]{0:T(1024)}, f32[24]{0:T(128)}, f32[24]{0:T(128)}, /*index=5*/f32[24]{0:T(128)}, f32[1536]{0:T(1024)}, f32[]{:T(128)}, f32[]{:T(128)}, f32[]{:T(128)}) all-reduce(f32[768]{0:T(1024)S(1)} %get-tuple-element.396, ...), channel_id=1, replica_groups=mesh['dp'=8,'seq'=4] {'dp','seq'}, use_global_device_ids=true, to_apply=%region_26.27 | all-reduce | flops 11339 | bytes 90712 | tf_op jit(solution)/shard_map/psum | solution.py:288
  877.1 2.7 broadcast_in_dim.133
  879.8 16.6 %dynamic_update_slice.12 = bf16[768,3352]{0,1:T(8,128)(2,1)} dynamic-update-slice(bf16[768,3352]{0,1:T(8,128)(2,1)} %broadcast_in_dim.133, bf16[192,3352]{0,1:T(8,128)(2,1)S(1)} %copy-done.12, s32[]{:T(128)S(6)} %select_n.153, s32[]{:T(128)} %constant.139.clone.1) | dynamic-update-slice | bytes 2574340 | tf_op jit(solution)/shard_map/dynamic_update_slice | solution.py:15
  896.3 4.9 copy.292
  902.7 2.7 copy.285
  905.4 17.9 %dynamic_update_slice.13 = bf16[768,3352]{0,1:T(8,128)(2,1)} dynamic-update-slice(bf16[768,3352]{0,1:T(8,128)(2,1)} %dynamic_update_slice.12, bf16[192,3352]{0,1:T(8,128)(2,1)S(1)} %copy.285, s32[]{:T(128)S(6)} %select_n.155, s32[]{:T(128)} %constant.139.clone.1) | dynamic-update-slice | bytes 2574340 | tf_op jit(solution)/shard_map/dynamic_update_slice | solution.py:20
  923.3 2.7 copy.287
  926.1 18.7 %dynamic_update_slice.14 = bf16[768,3352]{0,1:T(8,128)(2,1)} dynamic-update-slice(bf16[768,3352]{0,1:T(8,128)(2,1)} %dynamic_update_slice.13, bf16[192,3352]{0,1:T(8,128)(2,1)S(1)} %copy.287, s32[]{:T(128)S(6)} %select_n.157, s32[]{:T(128)} %constant.139.clone.1) | dynamic-update-slice | bytes 2574340 | tf_op jit(solution)/shard_map/dynamic_update_slice | solution.py:25
  944.8 2.7 copy.288
  947.5 16.2 %dynamic_update_slice.15 = bf16[768,3352]{0,1:T(8,128)(2,1)} dynamic-update-slice(bf16[768,3352]{0,1:T(8,128)(2,1)} %dynamic_update_slice.14, bf16[192,3352]{0,1:T(8,128)(2,1)S(1)} %copy.288, s32[]{:T(128)S(6)} %select_n.159, s32[]{:T(128)} %constant.139.clone.1) | dynamic-update-slice | bytes 2574340 | tf_op jit(solution)/shard_map/dynamic_update_slice | solution.py:20
  963.7 4.3 copy.291
  (312 shorter events, 64.6 us)
Async XLA Ops:
  7.2 87.7 %all-gather.8.cloned.1.call-start = ((), (), s32[]{:S(2)}) async-start(), calls=%async_computation.2 | async-start | bytes 1966080 | tf_op jit(solution)/shard_map/all_gather | solution.py:40
  9.2 5.6 copy-start.72
  9.2 10.6 %copy-start.76 = (s32[1,512]{1,0:T(1,128)S(1)}, s32[1,512]{1,0:T(1,128)}, u32[]{:S(2)}) copy-start(s32[1,512]{1,0:T(1,128)} %param.24) | copy-start | bytes 6148
  9.2 14.2 %copy-start.97 = (f32[24]{0:T(128)S(1)}, f32[24]{0:T(128)}, u32[]{:S(2)}) copy-start(f32[24]{0:T(128)} %param.34) | copy-start | bytes 292
  9.2 14.2 %copy-start.79 = (f32[24]{0:T(128)S(1)}, f32[24]{0:T(128)}, u32[]{:S(2)}) copy-start(f32[24]{0:T(128)} %param.33) | copy-start | bytes 292
  14.8 8.6 copy-start.4
  14.8 21.5 %collective-permute-start = (f32[1,3,1792]{2,0,1:T(1,128)S(1)}, f32[1,3,1792]{2,0,1:T(1,128)S(1)}, u32[]{:S(2)}, u32[]{:S(2)}) collective-permute-start(f32[1,3,1792]{2,0,1:T(1,128)S(1)} %copy.252), channel_id=1, source_target_pairs={{0,1},{1,2},{2,3},{4,5},{5,6},{6,7},{8,9},{9,10},{10,11},{12,13},{... | collective-permute-start | bytes 64520 | tf_op jit(solution)/shard_map/ppermute | solution.py:34
  19.9 16.3 %collective-permute-start.1 = (f32[1,3]{1,0:T(1,128)S(1)}, f32[1,3]{1,0:T(1,128)S(1)}, u32[]{:S(2)}, u32[]{:S(2)}) collective-permute-start(f32[1,3]{1,0:T(1,128)S(1)} %slice.135), channel_id=1, source_target_pairs={{0,1},{1,2},{2,3},{4,5},{5,6},{6,7},{8,9},{9,10},{10,11},{12,13},{... | collective-permute-start | bytes 44 | tf_op jit(solution)/shard_map/ppermute | solution.py:34
  25.8 10.2 %copy-start.66 = (f32[4,1792]{1,0:T(4,128)S(1)}, f32[4,1792]{1,0:T(4,128)}, u32[]{:S(2)}) copy-start(f32[4,1792]{1,0:T(4,128)} %param.31) | copy-start | bytes 86020
  25.8 10.5 %copy-start.78 = (f32[1792]{0:T(1024)S(1)}, f32[1792]{0:T(1024)}, u32[]{:S(2)}) copy-start(f32[1792]{0:T(1024)} %param.32) | copy-start | bytes 21508
  30.1 17.6 %copy-start.58 = (f32[1,512]{1,0:T(1,128)}, f32[1,512]{1,0:T(1,128)S(1)}, u32[]{:S(2)}) copy-start(f32[1,512]{1,0:T(1,128)S(1)} %compare_convert_fusion) | copy-start | bytes 6148
  30.9 16.8 %copy-start.65 = (s32[512]{0:T(512)}, s32[512]{0:T(512)S(1)}, u32[]{:S(2)}) copy-start(s32[512]{0:T(512)S(1)} %get-tuple-element.452) | copy-start | bytes 6148
  36.2 11.6 %copy-start.42 = (f32[1792]{0:T(1024)}, f32[1792]{0:T(1024)S(1)}, u32[]{:S(2)}) copy-start(f32[1792]{0:T(1024)S(1)} %get-tuple-element.401) | copy-start | bytes 21508
  36.2 11.6 %copy-start.44 = (f32[1792]{0:T(1024)}, f32[1792]{0:T(1024)S(1)}, u32[]{:S(2)}) copy-start(f32[1792]{0:T(1024)S(1)} %get-tuple-element.402) | copy-start | bytes 21508
  36.3 11.5 %copy-start.52 = (f32[1,512]{1,0:T(1,128)}, f32[1,512]{1,0:T(1,128)S(1)}, u32[]{:S(2)}) copy-start(f32[1,512]{1,0:T(1,128)S(1)} %get-tuple-element.470) | copy-start | bytes 6148
  36.3 11.5 %copy-start.54 = (f32[1,512]{1,0:T(1,128)}, f32[1,512]{1,0:T(1,128)S(1)}, u32[]{:S(2)}) copy-start(f32[1,512]{1,0:T(1,128)S(1)} %get-tuple-element.471) | copy-start | bytes 6148
  36.3 11.5 %copy-start.56 = (f32[1,512]{1,0:T(1,128)}, f32[1,512]{1,0:T(1,128)S(1)}, u32[]{:S(2)}) copy-start(f32[1,512]{1,0:T(1,128)S(1)} %get-tuple-element.472) | copy-start | bytes 6148
  58.4 212.3 %all-gather.10.cloned.1.call-start = ((), (), s32[]{:S(2)}) async-start(), calls=%async_computation.3 | async-start | bytes 3932160 | tf_op jit(solution)/shard_map/all_gather | solution.py:59
  100.2 29.4 %copy-start.14 = (f32[512,24,64]{0,2,1:T(8,128)}, f32[512,24,64]{0,2,1:T(8,128)S(1)}, u32[]{:S(2)}) copy-start(f32[512,24,64]{0,2,1:T(8,128)S(1)} %fusion.88) | copy-start | bytes 9437188
  141.2 7.3 copy-start.15
  163.1 5.5 copy-start.92
  168.6 446.4 %reduce-scatter.4.cloned.1.call-start = ((), (), s32[]{:S(2)}) async-start(), calls=%async_computation.5 | async-start | bytes 19169280
  230.6 11.1 %copy-start.20 = (f32[512,512]{1,0:T(8,128)S(1)}, f32[512,512]{1,0:T(8,128)}, u32[]{:S(2)}) copy-start(f32[512,512]{1,0:T(8,128)} %get-tuple-element.388) | copy-start | bytes 3145732
  230.6 13.7 %copy-start.7 = (f32[1,512,1536]{2,1,0:T(8,128)S(1)}, f32[1,512,1536]{2,1,0:T(8,128)}, u32[]{:S(2)}) copy-start(f32[1,512,1536]{2,1,0:T(8,128)} %copy-done.6) | copy-start | bytes 9437188
  230.6 13.7 %copy-start.18 = (bf16[1,512,768]{2,1,0:T(8,128)(2,1)S(1)}, bf16[1,512,768]{2,1,0:T(8,128)(2,1)}, u32[]{:S(2)}) copy-start(bf16[1,512,768]{2,1,0:T(8,128)(2,1)} %param.23) | copy-start | bytes 2359300
  230.6 13.7 %copy-start.49 = (f32[1536]{0:T(1024)S(1)}, f32[1536]{0:T(1024)}, u32[]{:S(2)}) copy-start(f32[1536]{0:T(1024)} %param.36) | copy-start | bytes 18436
  230.6 13.7 %copy-start.68 = (f32[512]{0:T(512)S(1)}, f32[512]{0:T(512)}, u32[]{:S(2)}) copy-start(f32[512]{0:T(512)} %copy-done.67) | copy-start | bytes 6148
  282.7 5.0 copy-start.32
  282.7 10.8 %copy-start.24 = (f32[24,64,512]{2,1,0:T(8,128)S(1)}, f32[24,64,512]{2,1,0:T(8,128)}, u32[]{:S(2)}) copy-start(f32[24,64,512]{2,1,0:T(8,128)} %fusion.2) | copy-start | bytes 9437188
  286.9 6.6 copy-start.11
  286.9 6.6 copy-start.40
  286.9 6.6 copy-start.95
  300.2 10.9 %copy-start.43 = (f32[1792]{0:T(1024)S(1)}, f32[1792]{0:T(1024)}, u32[]{:S(2)}) copy-start(f32[1792]{0:T(1024)} %copy-done.42) | copy-start | bytes 21508
  300.2 10.9 %copy-start.45 = (f32[1792]{0:T(1024)S(1)}, f32[1792]{0:T(1024)}, u32[]{:S(2)}) copy-start(f32[1792]{0:T(1024)} %copy-done.44) | copy-start | bytes 21508
  312.8 5.9 copy-start.91
  315.8 13.6 %copy-start.41 = (f32[512,24]{0,1:T(8,128)S(1)}, f32[512,24]{0,1:T(8,128)}, u32[]{:S(2)}) copy-start(f32[512,24]{0,1:T(8,128)} %get-tuple-element.466) | copy-start | bytes 147460
  315.8 15.8 %collective-permute-start.2 = (bf16[1,3,1792]{2,1,0:T(4,128)(2,1)S(1)}, bf16[1,3,1792]{2,1,0:T(4,128)(2,1)S(1)}, u32[]{:S(2)}, u32[]{:S(2)}) collective-permute-start(bf16[1,3,1792]{2,1,0:T(4,128)(2,1)S(1)} %slice.284), channel_id=1, source_target_pairs={{1,0},{2,1},{3,2},{5,4},{6,5},{7,6},{9,8},{10,9},{11,10},{13,12},{... | collective-permute-start | bytes 32264 | tf_op jit(solution)/shard_map/ppermute | solution.py:34
  329.6 4.6 copy-start.21
  329.6 4.6 copy-start.28
  329.6 4.6 copy-start.73
  329.6 4.6 copy-start.87
  331.6 5.7 slice-start
  358.4 353.9 %all-reduce.16.cloned.1.call-start = ((), (), s32[]{:S(2)}) async-start(), calls=%async_computation.4 | async-start | bytes 10010624 | tf_op jit(solution)/shard_map/psum | solution.py:262
  620.7 342.9 %all-gather.6.cloned.1.call-start = ((), (), s32[]{:S(2)}) async-start(), calls=%async_computation.1 | async-start | bytes 2949120 | tf_op jit(solution)/shard_map/all_gather | solution.py:275
  716.8 12.8 %copy-start.51 = (f32[1536]{0:T(1024)S(1)}, f32[1536]{0:T(1024)}, u32[]{:S(2)}) copy-start(f32[1536]{0:T(1024)} %get-tuple-element.436) | copy-start | bytes 18436
  716.8 13.0 %copy-start.8 = (f32[1,512,1536]{2,1,0:T(8,128)S(1)}, f32[1,512,1536]{2,1,0:T(8,128)}, u32[]{:S(2)}) copy-start(f32[1,512,1536]{2,1,0:T(8,128)} %copy-done.6) | copy-start | bytes 9437188
  716.8 13.0 %copy-start.50 = (f32[1536]{0:T(1024)S(1)}, f32[1536]{0:T(1024)}, u32[]{:S(2)}) copy-start(f32[1536]{0:T(1024)} %param.36) | copy-start | bytes 18436
  716.9 13.0 %copy-start.69 = (f32[512]{0:T(512)S(1)}, f32[512]{0:T(512)}, u32[]{:S(2)}) copy-start(f32[512]{0:T(512)} %copy-done.67) | copy-start | bytes 6148
  728.1 62.5 %collective-permute-start.3 = (bf16[192,3352]{1,0:T(8,128)(2,1)}, bf16[192,3352]{1,0:T(8,128)(2,1)}, u32[]{:S(2)}, u32[]{:S(2)}) collective-permute-start(bf16[192,3352]{1,0:T(8,128)(2,1)} %copy.284), channel_id=1, source_target_pairs={{0,1},{1,2},{2,3},{3,0},{4,5},{5,6},{6,7},{7,4},{8,9},{9,10},{10,1... | collective-permute-start | bytes 3861512 | tf_op jit(solution)/shard_map/ppermute | solution.py:19
  729.9 75.9 %copy-start.22 = (bf16[1,512,768]{2,1,0:T(8,128)(2,1)S(1)}, bf16[1,512,768]{2,1,0:T(8,128)(2,1)}, u32[]{:S(2)}) copy-start(bf16[1,512,768]{2,1,0:T(8,128)(2,1)} %param.22) | copy-start | bytes 2359300
  729.9 75.9 %copy-start.27 = (bf16[512,1792]{1,0:T(8,128)(2,1)S(1)}, bf16[512,1792]{1,0:T(8,128)(2,1)}, u32[]{:S(2)}) copy-start(bf16[512,1792]{1,0:T(8,128)(2,1)} %copy-done.26) | copy-start | bytes 5505028
  729.9 75.9 %copy-start.29 = (bf16[512,1536]{1,0:T(8,128)(2,1)S(1)}, bf16[512,1536]{1,0:T(8,128)(2,1)}, u32[]{:S(2)}) copy-start(bf16[512,1536]{1,0:T(8,128)(2,1)} %get-tuple-element.457) | copy-start | bytes 4718596
  730.0 75.8 %copy-start.74 = (f32[512]{0:T(512)S(1)}, f32[512]{0:T(512)}, u32[]{:S(2)}) copy-start(f32[512]{0:T(512)} %copy-done.72) | copy-start | bytes 6148
  730.0 75.8 %copy-start.88 = (f32[768]{0:T(1024)S(1)}, f32[768]{0:T(1024)}, u32[]{:S(2)}) copy-start(f32[768]{0:T(1024)} %param.29) | copy-start | bytes 9220
  733.5 189.8 %collective-permute-start.4 = (bf16[192,3352]{1,0:T(8,128)(2,1)}, bf16[192,3352]{1,0:T(8,128)(2,1)}, u32[]{:S(2)}, u32[]{:S(2)}) collective-permute-start(bf16[192,3352]{1,0:T(8,128)(2,1)} %copy.284), channel_id=1, source_target_pairs={{0,3},{1,0},{2,1},{3,2},{4,7},{5,4},{6,5},{7,6},{8,11},{9,8},{10,9... | collective-permute-start | bytes 3861512 | tf_op jit(solution)/shard_map/ppermute | solution.py:24
  790.6 154.2 %collective-permute-start.5 = (bf16[192,3352]{1,0:T(8,128)(2,1)}, bf16[192,3352]{1,0:T(8,128)(2,1)}, u32[]{:S(2)}, u32[]{:S(2)}) collective-permute-start(bf16[192,3352]{1,0:T(8,128)(2,1)} %collective-permute-done.3), channel_id=1, source_target_pairs={{0,1},{1,2},{2,3},{3,0},{4,5},{5,6},{6,7},{7,4},{8,9},{9,10},{10,1... | collective-permute-start | bytes 3861512 | tf_op jit(solution)/shard_map/ppermute | solution.py:19
  805.8 6.8 copy-start.77
  805.8 7.4 copy-start.60
  805.8 7.4 copy-start.75
  805.8 7.4 copy-start.90
  805.9 69.8 %copy-start.71 = (f32[512]{0:T(512)S(1)}, f32[512]{0:T(512)}, u32[]{:S(2)}) copy-start(f32[512]{0:T(512)} %copy-done.70) | copy-start | bytes 6148
  805.9 69.8 %copy-start.19 = (bf16[1,512,768]{2,1,0:T(8,128)(2,1)S(1)}, bf16[1,512,768]{2,1,0:T(8,128)(2,1)}, u32[]{:S(2)}) copy-start(bf16[1,512,768]{2,1,0:T(8,128)(2,1)} %param.23) | copy-start | bytes 2359300
  805.9 69.8 %copy-start.23 = (bf16[1,512,768]{2,1,0:T(8,128)(2,1)S(1)}, bf16[1,512,768]{2,1,0:T(8,128)(2,1)}, u32[]{:S(2)}) copy-start(bf16[1,512,768]{2,1,0:T(8,128)(2,1)} %param.22) | copy-start | bytes 2359300
  896.3 4.9 copy-start.16
  (48 other events, 158.5 us)
Sparse Core Ops, SparseCore 0:
  58.5 36.3 all-gather.7
  168.7 71.0 all-gather.9
  358.5 256.4 reduce-scatter.3
  620.8 91.3 all-reduce.15
  716.9 94.3 all-gather.5
